TPU v7x, 512 devices: a whole 4x4x16 slice. The times are simulated.
512 devices in a mesh: bl: 32 (over y, x, core), dir: 16 (over z).
Axes of the slice: x: 4, y: 4, z: 16, core: 2. Of those that a mesh axis runs over, the one named last changes fastest.
Arguments:
- visibilities: float32 [8, 16, 8192], P(None, 'dir', 'bl'), may hold values from -24 to 24
- coherencies: bfloat16 [32, 8, 16, 8192], P('dir', None, None, 'bl'), may hold values from -6 to 6
- gain_offsets: float32 [32, 8, 512], P(None, None, 'bl'), may hold values from -1.5 to 1.5
- stations: int32 [2, 8192], P(None, 'bl'), may hold values from 0 to 511, as said below
- solve_order: int32 [32], replicated, may hold values from 0 to 31, each once
- counts: int32 [32], replicated, may hold values from 1 to 2
- damping: int32 [32], replicated, may hold values from 1 to 8
Outputs:
- gains: float32 [32, 8, 512], P(None, None, 'bl')
- residual: float32 [8, 16, 8192], P(None, 'dir', 'bl')
Inputs may be any that keep to these rules, and one draw needn't show every extreme that they name: Each baseline names two different stations. `solve_order`: each direction appears once.
All inputs are finite; a program needn't handle non-finite values.
Results may differ from a plain program's by a relative error of at most 0.0003.
Values may be sent and summed in bfloat16 or wider, within the bound.
A program may use at most 64 MiB of HBM per device.

v0:
```python
import jax
import jax.numpy as jnp
from jax import lax
from jax.sharding import PartitionSpec as P

LM_ITERS = 2
SOLVED = 4


def matrix_entry(mat, i, j):
    return (mat[4 * i + 2 * j], mat[4 * i + 2 * j + 1])


def matmul_two(left, right):
    pieces = []
    for i in (0, 1):
        for j in (0, 1):
            left_r0, left_i0 = matrix_entry(left, i, 0)
            left_r1, left_i1 = matrix_entry(left, i, 1)
            right_r0, right_i0 = matrix_entry(right, 0, j)
            right_r1, right_i1 = matrix_entry(right, 1, j)
            pieces.append(
                left_r0 * right_r0 - left_i0 * right_i0 + left_r1 * right_r1 - left_i1 * right_i1
            )
            pieces.append(
                left_r0 * right_i0 + left_i0 * right_r0 + left_r1 * right_i1 + left_i1 * right_r1
            )
    return jnp.stack(pieces)


def adjoint(mat):
    return jnp.stack([mat[0], -mat[1], mat[4], -mat[5], mat[2], -mat[3], mat[6], -mat[7]])


def apply_gains(gain_p, coher_now, gain_q):
    return matmul_two(matmul_two(gain_p, coher_now), adjoint(gain_q))


def gram_parts(gram):
    return jnp.stack([gram[0], gram[6], gram[2], gram[3]])


def station_terms(gain_p, gain_q, coher_now, target):
    z_rows = matmul_two(coher_now, adjoint(gain_q))
    y_rows = matmul_two(adjoint(coher_now), adjoint(gain_p))
    leading_endpoint = jnp.concatenate(
        [matmul_two(target, adjoint(z_rows)), gram_parts(matmul_two(z_rows, adjoint(z_rows)))], 0
    )
    second = jnp.concatenate(
        [
            matmul_two(adjoint(target), adjoint(y_rows)),
            gram_parts(matmul_two(y_rows, adjoint(y_rows))),
        ],
        0,
    )
    return (jnp.sum(leading_endpoint, axis=1), jnp.sum(second, axis=1))


def solve_station(gathered_sums, gain_now, damp_value):
    numerator = gathered_sums[:8] + damp_value * gain_now
    diag_a = gathered_sums[8] + damp_value
    diag_d = gathered_sums[9] + damp_value
    cross_r = gathered_sums[10]
    cross_i = gathered_sums[11]
    determinant = diag_a * diag_d - cross_r * cross_r - cross_i * cross_i
    zeros_row = jnp.zeros_like(determinant)
    inverse = (
        jnp.stack([diag_d, zeros_row, -cross_r, -cross_i, -cross_r, cross_i, diag_a, zeros_row])
        / determinant
    )
    return matmul_two(numerator, inverse)


def on_device(visibilities, coherencies, gain_offsets, stations, solve_order, counts, damping):
    identity = jnp.zeros((8,), jnp.float32).at[0].set(1.0).at[6].set(1.0)
    start = lax.all_gather(gain_offsets, "bl", axis=2, tiled=True) + identity[None, :, None]
    groups = lax.axis_size("bl")
    total_channels = coherencies.shape[2]
    station_count = start.shape[2]
    damping_factor = visibilities.shape[2] * groups * total_channels / station_count
    coher_all = lax.all_to_all(coherencies, "dir", 2, 0, tiled=True)
    ends_p = jnp.take(start, stations[0], axis=2)
    ends_q = jnp.take(start, stations[1], axis=2)
    gain_p = jnp.transpose(ends_p, (1, 0, 2))[:, :, None, :]
    gain_q = jnp.transpose(ends_q, (1, 0, 2))[:, :, None, :]
    coher_f32 = jnp.transpose(coher_all, (1, 0, 2, 3)).astype(jnp.float32)
    first_model = jnp.sum(apply_gains(gain_p, coher_f32, gain_q), axis=1)
    first_residual = visibilities - first_model

    def direction_model(gain_now, coher_now):
        gain_p = jnp.take(gain_now, stations[0], axis=1)[:, None, :]
        gain_q = jnp.take(gain_now, stations[1], axis=1)[:, None, :]
        return apply_gains(gain_p, coher_now, gain_q)

    def sweep(step_index, state):
        gain_table, residual = state
        which = solve_order[step_index]
        coher_now = lax.dynamic_index_in_dim(coher_all, which, 0, keepdims=False).astype(
            jnp.float32
        )
        damp_value = damping[which].astype(jnp.float32) * damping_factor
        gain_start = gain_table[which]
        target = residual + direction_model(gain_start, coher_now)

        def iterate(round_index, gain_now):
            gain_p = jnp.take(gain_now, stations[0], axis=1)[:, None, :]
            gain_q = jnp.take(gain_now, stations[1], axis=1)[:, None, :]
            leading_endpoint, second = station_terms(gain_p, gain_q, coher_now, target)
            local_sums = (
                jax.ops.segment_sum(leading_endpoint.T, stations[0], station_count)
                + jax.ops.segment_sum(second.T, stations[1], station_count)
            ).T
            gathered_sums = lax.psum(local_sums, ("bl", "dir"))
            return solve_station(gathered_sums, gain_now, damp_value)

        rounds = jnp.clip(counts[which], 0, LM_ITERS)
        gain_final = lax.fori_loop(0, rounds, iterate, gain_start)
        residual = target - direction_model(gain_final, coher_now)
        return (gain_table.at[which].set(gain_final), residual)

    gain_table, residual = lax.fori_loop(0, SOLVED, sweep, (start, first_residual))
    own_width = station_count // groups
    gains = lax.dynamic_slice_in_dim(gain_table, lax.axis_index("bl") * own_width, own_width, 2)
    return (gains, residual)


def solution(mesh):
    return jax.shard_map(
        on_device,
        mesh=mesh,
        in_specs=(
            P(None, "dir", "bl"),
            P("dir", None, None, "bl"),
            P(None, None, "bl"),
            P(None, "bl"),
            P(),
            P(),
            P(),
        ),
        out_specs=(P(None, None, "bl"), P(None, "dir", "bl")),
        check_vma=False,
    )
```

profile of v0, /device:TPU:1, one launch (start us, length us, event | category | flops | bytes accessed | tf_op | source)
XLA Modules:
  0.0 847.1 jit_solution(9811879134477437065)
XLA Ops:
  0.6 1.6 copy.1122
  2.2 15.7 %all-to-all-start = ((bf16[2,8,16,256]{3,1,0,2:T(8,128)(2,1)}), bf16[2,8,16,256]{3,1,0,2:T(8,128)(2,1)S(1)}, u32[]{:S(2)}, u32[]{:S(2)}) async-start(bf16[2,8,16,256]{3,1,0,2:T(8,128)(2,1)} %copy.1122), calls=%async_computation | async-start | bytes 262144 | tf_op jit(solution)/shard_map/all_to_all | solution.py:81
  19.7 27.2 %all_gather.3 = f32[32,8,512]{0,1,2:T(8,128)S(1)} all-gather(f32[32,8,16]{0,1,2:T(8,128)S(1)} %copy.1120), channel_id=1, replica_groups=mesh['bl'=32,'dir'=16] {'bl'}, dimensions={2}, use_global_device_ids=true | all-gather | bytes 540672 | tf_op jit(solution)/shard_map/all_gather | solution.py:76
  48.0 2.0 gather_fusion.7
  50.0 1.6 copy.1124
  51.6 2.0 gather_fusion.6
  53.6 1.6 copy.1121
  57.4 788.4 %while.42 = (s32[]{:T(128)}, f32[32,8,512]{2,1,0:T(8,128)S(1)}, f32[8,1,256]{2,1,0:T(1,128)S(1)}, s32[32]{0:T(128)S(1)}, s32[32]{0:T(128)S(1)}, /*index=5*/bf16[...) while((s32[]{:T(128)}, f32[32,8,512]{2,1,0:T(8,128)S(1)}, ...), condition=%wide.region_8.12_spmd, body=%wide.region_1.11_spmd.sunk | while | flops 253464 | bytes 1958014 | solution.py:121
  64.8 109.2 %while.43 = (s32[]{:T(128)}, f32[8,512]{1,0:T(8,128)S(1)}, s32[]{:T(128)}, s32[2,256]{1,0:T(2,128)S(1)}, f32[8,1,256]{2,1,0:T(1,128)S(1)}, /*index=5*/f32[8,1,25...) while((s32[]{:T(128)}, f32[8,512]{1,0:T(8,128)S(1)}, ...), condition=%wide.region_7.10_spmd, body=%wide.region_3.9_spmd.sunk | while | flops 160768 | bytes 1263793 | solution.py:117
  67.0 1.5 scatter_custom_fusion.11
  69.0 1.5 scatter_custom_fusion.10
  70.6 103.1 %psum.9 = f32[12,512]{1,0:T(8,128)S(1)} all-reduce(f32[12,512]{1,0:T(8,128)S(1)} %add_bitcast_fusion.2), channel_id=1, replica_groups=mesh['bl'=32,'dir'=16] {'bl','dir'}, use_global_device_ids=true, to_apply=%region_6.8 | all-reduce | flops 6144 | bytes 49152 | tf_op jit(solution)/shard_map/while/body/eval_jaxpr/while/body/psum | solution.py:113
  184.6 212.3 %while.43 = (s32[]{:T(128)}, f32[8,512]{1,0:T(8,128)S(1)}, s32[]{:T(128)}, s32[2,256]{1,0:T(2,128)S(1)}, f32[8,1,256]{2,1,0:T(1,128)S(1)}, /*index=5*/f32[8,1,25...) while((s32[]{:T(128)}, f32[8,512]{1,0:T(8,128)S(1)}, ...), condition=%wide.region_7.10_spmd, body=%wide.region_3.9_spmd.sunk | while | flops 160768 | bytes 1263793 | solution.py:117
  186.8 1.5 scatter_custom_fusion.11
  188.8 1.5 scatter_custom_fusion.10
  190.4 100.7 %psum.9 = f32[12,512]{1,0:T(8,128)S(1)} all-reduce(f32[12,512]{1,0:T(8,128)S(1)} %add_bitcast_fusion.2), channel_id=1, replica_groups=mesh['bl'=32,'dir'=16] {'bl','dir'}, use_global_device_ids=true, to_apply=%region_6.8 | all-reduce | flops 6144 | bytes 49152 | tf_op jit(solution)/shard_map/while/body/eval_jaxpr/while/body/psum | solution.py:113
  293.6 1.5 scatter_custom_fusion.11
  295.5 1.5 scatter_custom_fusion.10
  297.2 99.4 %psum.9 = f32[12,512]{1,0:T(8,128)S(1)} all-reduce(f32[12,512]{1,0:T(8,128)S(1)} %add_bitcast_fusion.2), channel_id=1, replica_groups=mesh['bl'=32,'dir'=16] {'bl','dir'}, use_global_device_ids=true, to_apply=%region_6.8 | all-reduce | flops 6144 | bytes 49152 | tf_op jit(solution)/shard_map/while/body/eval_jaxpr/while/body/psum | solution.py:113
  407.5 212.1 %while.43 = (s32[]{:T(128)}, f32[8,512]{1,0:T(8,128)S(1)}, s32[]{:T(128)}, s32[2,256]{1,0:T(2,128)S(1)}, f32[8,1,256]{2,1,0:T(1,128)S(1)}, /*index=5*/f32[8,1,25...) while((s32[]{:T(128)}, f32[8,512]{1,0:T(8,128)S(1)}, ...), condition=%wide.region_7.10_spmd, body=%wide.region_3.9_spmd.sunk | while | flops 160768 | bytes 1263793 | solution.py:117
  409.7 1.5 scatter_custom_fusion.11
  411.7 1.5 scatter_custom_fusion.10
  413.3 100.4 %psum.9 = f32[12,512]{1,0:T(8,128)S(1)} all-reduce(f32[12,512]{1,0:T(8,128)S(1)} %add_bitcast_fusion.2), channel_id=1, replica_groups=mesh['bl'=32,'dir'=16] {'bl','dir'}, use_global_device_ids=true, to_apply=%region_6.8 | all-reduce | flops 6144 | bytes 49152 | tf_op jit(solution)/shard_map/while/body/eval_jaxpr/while/body/psum | solution.py:113
  516.2 1.5 scatter_custom_fusion.11
  518.1 1.5 scatter_custom_fusion.10
  519.7 99.6 %psum.9 = f32[12,512]{1,0:T(8,128)S(1)} all-reduce(f32[12,512]{1,0:T(8,128)S(1)} %add_bitcast_fusion.2), channel_id=1, replica_groups=mesh['bl'=32,'dir'=16] {'bl','dir'}, use_global_device_ids=true, to_apply=%region_6.8 | all-reduce | flops 6144 | bytes 49152 | tf_op jit(solution)/shard_map/while/body/eval_jaxpr/while/body/psum | solution.py:113
  630.2 212.2 %while.43 = (s32[]{:T(128)}, f32[8,512]{1,0:T(8,128)S(1)}, s32[]{:T(128)}, s32[2,256]{1,0:T(2,128)S(1)}, f32[8,1,256]{2,1,0:T(1,128)S(1)}, /*index=5*/f32[8,1,25...) while((s32[]{:T(128)}, f32[8,512]{1,0:T(8,128)S(1)}, ...), condition=%wide.region_7.10_spmd, body=%wide.region_3.9_spmd.sunk | while | flops 160768 | bytes 1263793 | solution.py:117
  632.5 1.5 scatter_custom_fusion.11
  634.4 1.5 scatter_custom_fusion.10
  636.0 100.5 %psum.9 = f32[12,512]{1,0:T(8,128)S(1)} all-reduce(f32[12,512]{1,0:T(8,128)S(1)} %add_bitcast_fusion.2), channel_id=1, replica_groups=mesh['bl'=32,'dir'=16] {'bl','dir'}, use_global_device_ids=true, to_apply=%region_6.8 | all-reduce | flops 6144 | bytes 49152 | tf_op jit(solution)/shard_map/while/body/eval_jaxpr/while/body/psum | solution.py:113
  739.0 1.5 scatter_custom_fusion.11
  742.5 99.6 %psum.9 = f32[12,512]{1,0:T(8,128)S(1)} all-reduce(f32[12,512]{1,0:T(8,128)S(1)} %add_bitcast_fusion.2), channel_id=1, replica_groups=mesh['bl'=32,'dir'=16] {'bl','dir'}, use_global_device_ids=true, to_apply=%region_6.8 | all-reduce | flops 6144 | bytes 49152 | tf_op jit(solution)/shard_map/while/body/eval_jaxpr/while/body/psum | solution.py:113
  (595 shorter events, 56.4 us)
Async XLA Ops:
  0.6 46.2 %copy-start.4 = (f32[8]{0:T(128)S(1)}, f32[8]{0:T(128)}, u32[]{:S(2)}) copy-start(f32[8]{0:T(128)} %constant.188.clone.1) | copy-start | bytes 100
  2.2 53.1 %all-to-all-start = ((bf16[2,8,16,256]{3,1,0,2:T(8,128)(2,1)}), bf16[2,8,16,256]{3,1,0,2:T(8,128)(2,1)S(1)}, u32[]{:S(2)}, u32[]{:S(2)}) async-start(bf16[2,8,16,256]{3,1,0,2:T(8,128)(2,1)} %copy.1122), calls=%async_computation | async-start | bytes 262144 | tf_op jit(solution)/shard_map/all_to_all | solution.py:81
  55.2 2.1 copy-start.3
  55.2 2.1 copy-start
  55.3 2.1 copy-start.2
  55.3 2.1 copy-start.5
  55.3 2.1 copy-start.6
  55.3 2.1 copy-start.7
  845.8 1.3 copy-start.1
where the time goes:
time: 849 us; the launch traced here: 847 us
  blocking collectives  731 us (86%)
  local copies, waits for them, and re-layouts  49.5 us (6%)
  other arithmetic  35.1 us (4%)
  starting transfers between devices  15.7 us (2%)
  loops' own time  15.3 us (2%)
    psum x7, blocking collectives, iterate(): gathered_sums = lax.psum(local_sums, ('bl', 'dir'))  703 us
    all_gather x1, blocking collectives, on_device(): lax.all_gather(gain_offsets, 'bl', axis=2, tiled=True)  27.2 us
  transfers between devices with their start and end apart: 1, of which 0 were waited for; matrix products, arithmetic and copies ran while one was open for 1% of the time, Pallas kernels for 0%

commit v1 on v0

--- a/solution.py
+++ b/solution.py
@@ -73,7 +73,12 @@
 
 def on_device(visibilities, coherencies, gain_offsets, stations, solve_order, counts, damping):
     identity = jnp.zeros((8,), jnp.float32).at[0].set(1.0).at[6].set(1.0)
-    start = lax.all_gather(gain_offsets, "bl", axis=2, tiled=True) + identity[None, :, None]
+    start = (
+        jnp.concatenate(
+            lax.all_to_all(jnp.stack([gain_offsets] * lax.axis_size("bl")), "bl", 0, 0), axis=2
+        )
+        + identity[None, :, None]
+    )
     groups = lax.axis_size("bl")
     total_channels = coherencies.shape[2]
     station_count = start.shape[2]

time: 849 us -> 856 us (level)
  blocking collectives: 731 us -> 700 us
  waiting for transfers between devices: 0.01 us -> 19.9 us
  starting transfers between devices: 15.7 us -> 26.5 us
    all_gather x1 -> x0, blocking collectives: 27.2 us -> none  [on_device(): lax.all_gather(gain_offsets, 'bl', axis=2, tiled=True)]
    all_to_all x0 -> x1, waiting for transfers between devices: none -> 11.5 us  [on_device(): lax.all_to_all(jnp.stack([gain_offsets] * lax.axis_size('bl')), 'bl', 0, 0)]
    all_to_all x0 -> x1, starting transfers between devices: none -> 10.7 us  [on_device(): lax.all_to_all(jnp.stack([gain_offsets] * lax.axis_size('bl')), 'bl', 0, 0)]
  transfers between devices with their start and end apart: 1 -> 2, of which waited for: 0 -> 2; matrix products, arithmetic and copies ran while one was open for 1% -> 0% of each run, Pallas kernels for 0% -> 0%
where the time goes in v1:
time: 856 us; the launch traced here: 855 us
  blocking collectives  700 us (82%)
  local copies, waits for them, and re-layouts  54 us (6%)
  other arithmetic  38.1 us (4%)
  starting transfers between devices  26.5 us (3%)
  waiting for transfers between devices  19.9 us (2%)
  loops' own time  15.6 us (2%)
    psum x7, blocking collectives, iterate(): gathered_sums = lax.psum(local_sums, ('bl', 'dir'))  700 us
  transfers between devices with their start and end apart: 2, of which 2 were waited for; matrix products, arithmetic and copies ran while one was open for 0% of the time, Pallas kernels for 0%

profile of v1, /device:TPU:1, one launch (start us, length us, event | category | flops | bytes accessed | tf_op | source)
XLA Modules:
  0.0 854.6 jit_solution(10953499605467925939)
XLA Ops:
  0.6 1.6 copy.1122
  2.2 15.7 %all-to-all-start.1 = ((bf16[2,8,16,256]{3,1,0,2:T(8,128)(2,1)}), bf16[2,8,16,256]{3,1,0,2:T(8,128)(2,1)S(1)}, u32[]{:S(2)}, u32[]{:S(2)}) async-start(bf16[2,8,16,256]{3,1,0,2:T(8,128)(2,1)} %copy.1122), calls=%async_computation.1 | async-start | bytes 262144 | tf_op jit(solution)/shard_map/all_to_all | solution.py:86
  19.9 1.7 reshape.1389
  21.6 8.4 all-to-all-done.1
  30.0 10.7 %all-to-all-start = ((f32[32,1,4096]{2,1,0:T(1,128)}), f32[32,1,4096]{2,1,0:T(1,128)S(1)}, u32[]{:S(2)}, u32[]{:S(2)}) async-start(f32[32,1,4096]{2,1,0:T(1,128)} %reshape.1389), calls=%async_computation | async-start | bytes 1048576 | tf_op jit(solution)/shard_map/all_to_all | solution.py:78
  40.8 11.5 %all-to-all-done = f32[32,1,4096]{2,1,0:T(1,128)S(1)} async-done(((f32[32,1,4096]{2,1,0:T(1,128)}), f32[32,1,4096]{2,1,0:T(1,128)S(1)}, u32[]{:S(2)}, u32[]{:S(2)}) %all-to-all-start) | async-done | bytes 524320 | tf_op jit(solution)/shard_map/all_to_all | solution.py:78
  52.8 1.9 reduce.16
  54.7 2.0 reshape.1390
  56.8 1.8 bitcast_add_fusion
  58.6 2.0 gather_fusion.7
  60.6 1.6 copy.1124
  62.1 2.0 gather_fusion.6
  64.2 1.6 copy.1121
  68.8 784.5 %while.42 = (s32[]{:T(128)}, f32[32,8,512]{2,1,0:T(8,128)S(1)}, f32[8,1,256]{2,1,0:T(1,128)S(1)}, s32[32]{0:T(128)S(1)}, s32[32]{0:T(128)S(1)}, /*index=5*/bf16[...) while((s32[]{:T(128)}, f32[32,8,512]{2,1,0:T(8,128)S(1)}, ...), condition=%wide.region_8.12_spmd, body=%wide.region_1.11_spmd.sunk | while | flops 253464 | bytes 1958014 | solution.py:126
  76.2 106.5 %while.43 = (s32[]{:T(128)}, f32[8,512]{1,0:T(8,128)S(1)}, s32[]{:T(128)}, s32[2,256]{1,0:T(2,128)S(1)}, f32[8,1,256]{2,1,0:T(1,128)S(1)}, /*index=5*/f32[8,1,25...) while((s32[]{:T(128)}, f32[8,512]{1,0:T(8,128)S(1)}, ...), condition=%wide.region_7.10_spmd, body=%wide.region_3.9_spmd.sunk | while | flops 160768 | bytes 1263793 | solution.py:122
  78.5 1.5 scatter_custom_fusion.11
  80.4 1.5 scatter_custom_fusion.10
  82.0 100.4 %psum.9 = f32[12,512]{1,0:T(8,128)S(1)} all-reduce(f32[12,512]{1,0:T(8,128)S(1)} %add_bitcast_fusion.2), channel_id=1, replica_groups=mesh['bl'=32,'dir'=16] {'bl','dir'}, use_global_device_ids=true, to_apply=%region_6.8 | all-reduce | flops 6144 | bytes 49152 | tf_op jit(solution)/shard_map/while/body/eval_jaxpr/while/body/psum | solution.py:118
  193.3 211.4 %while.43 = (s32[]{:T(128)}, f32[8,512]{1,0:T(8,128)S(1)}, s32[]{:T(128)}, s32[2,256]{1,0:T(2,128)S(1)}, f32[8,1,256]{2,1,0:T(1,128)S(1)}, /*index=5*/f32[8,1,25...) while((s32[]{:T(128)}, f32[8,512]{1,0:T(8,128)S(1)}, ...), condition=%wide.region_7.10_spmd, body=%wide.region_3.9_spmd.sunk | while | flops 160768 | bytes 1263793 | solution.py:122
  199.1 98.9 %psum.9 = f32[12,512]{1,0:T(8,128)S(1)} all-reduce(f32[12,512]{1,0:T(8,128)S(1)} %add_bitcast_fusion.2), channel_id=1, replica_groups=mesh['bl'=32,'dir'=16] {'bl','dir'}, use_global_device_ids=true, to_apply=%region_6.8 | all-reduce | flops 6144 | bytes 49152 | tf_op jit(solution)/shard_map/while/body/eval_jaxpr/while/body/psum | solution.py:118
  300.5 1.5 scatter_custom_fusion.11
  302.4 1.5 scatter_custom_fusion.10
  304.1 100.3 %psum.9 = f32[12,512]{1,0:T(8,128)S(1)} all-reduce(f32[12,512]{1,0:T(8,128)S(1)} %add_bitcast_fusion.2), channel_id=1, replica_groups=mesh['bl'=32,'dir'=16] {'bl','dir'}, use_global_device_ids=true, to_apply=%region_6.8 | all-reduce | flops 6144 | bytes 49152 | tf_op jit(solution)/shard_map/while/body/eval_jaxpr/while/body/psum | solution.py:118
  415.2 212.1 %while.43 = (s32[]{:T(128)}, f32[8,512]{1,0:T(8,128)S(1)}, s32[]{:T(128)}, s32[2,256]{1,0:T(2,128)S(1)}, f32[8,1,256]{2,1,0:T(1,128)S(1)}, /*index=5*/f32[8,1,25...) while((s32[]{:T(128)}, f32[8,512]{1,0:T(8,128)S(1)}, ...), condition=%wide.region_7.10_spmd, body=%wide.region_3.9_spmd.sunk | while | flops 160768 | bytes 1263793 | solution.py:122
  421.0 99.5 %psum.9 = f32[12,512]{1,0:T(8,128)S(1)} all-reduce(f32[12,512]{1,0:T(8,128)S(1)} %add_bitcast_fusion.2), channel_id=1, replica_groups=mesh['bl'=32,'dir'=16] {'bl','dir'}, use_global_device_ids=true, to_apply=%region_6.8 | all-reduce | flops 6144 | bytes 49152 | tf_op jit(solution)/shard_map/while/body/eval_jaxpr/while/body/psum | solution.py:118
  524.9 1.5 scatter_custom_fusion.10
  526.6 100.5 %psum.9 = f32[12,512]{1,0:T(8,128)S(1)} all-reduce(f32[12,512]{1,0:T(8,128)S(1)} %add_bitcast_fusion.2), channel_id=1, replica_groups=mesh['bl'=32,'dir'=16] {'bl','dir'}, use_global_device_ids=true, to_apply=%region_6.8 | all-reduce | flops 6144 | bytes 49152 | tf_op jit(solution)/shard_map/while/body/eval_jaxpr/while/body/psum | solution.py:118
  637.9 212.1 %while.43 = (s32[]{:T(128)}, f32[8,512]{1,0:T(8,128)S(1)}, s32[]{:T(128)}, s32[2,256]{1,0:T(2,128)S(1)}, f32[8,1,256]{2,1,0:T(1,128)S(1)}, /*index=5*/f32[8,1,25...) while((s32[]{:T(128)}, f32[8,512]{1,0:T(8,128)S(1)}, ...), condition=%wide.region_7.10_spmd, body=%wide.region_3.9_spmd.sunk | while | flops 160768 | bytes 1263793 | solution.py:122
  643.6 99.6 %psum.9 = f32[12,512]{1,0:T(8,128)S(1)} all-reduce(f32[12,512]{1,0:T(8,128)S(1)} %add_bitcast_fusion.2), channel_id=1, replica_groups=mesh['bl'=32,'dir'=16] {'bl','dir'}, use_global_device_ids=true, to_apply=%region_6.8 | all-reduce | flops 6144 | bytes 49152 | tf_op jit(solution)/shard_map/while/body/eval_jaxpr/while/body/psum | solution.py:118
  745.7 1.5 scatter_custom_fusion.11
  747.7 1.5 scatter_custom_fusion.10
  749.3 100.5 %psum.9 = f32[12,512]{1,0:T(8,128)S(1)} all-reduce(f32[12,512]{1,0:T(8,128)S(1)} %add_bitcast_fusion.2), channel_id=1, replica_groups=mesh['bl'=32,'dir'=16] {'bl','dir'}, use_global_device_ids=true, to_apply=%region_6.8 | all-reduce | flops 6144 | bytes 49152 | tf_op jit(solution)/shard_map/while/body/eval_jaxpr/while/body/psum | solution.py:118
  (601 shorter events, 65.4 us)
Async XLA Ops:
  2.2 27.8 %all-to-all-start.1 = ((bf16[2,8,16,256]{3,1,0,2:T(8,128)(2,1)}), bf16[2,8,16,256]{3,1,0,2:T(8,128)(2,1)S(1)}, u32[]{:S(2)}, u32[]{:S(2)}) async-start(bf16[2,8,16,256]{3,1,0,2:T(8,128)(2,1)} %copy.1122), calls=%async_computation.1 | async-start | bytes 262144 | tf_op jit(solution)/shard_map/all_to_all | solution.py:86
  30.0 22.3 %all-to-all-start = ((f32[32,1,4096]{2,1,0:T(1,128)}), f32[32,1,4096]{2,1,0:T(1,128)S(1)}, u32[]{:S(2)}, u32[]{:S(2)}) async-start(f32[32,1,4096]{2,1,0:T(1,128)} %reshape.1389), calls=%async_computation | async-start | bytes 1048576 | tf_op jit(solution)/shard_map/all_to_all | solution.py:78
  40.7 16.0 %copy-start.4 = (f32[8]{0:T(128)S(1)}, f32[8]{0:T(128)}, u32[]{:S(2)}) copy-start(f32[8]{0:T(128)} %constant.188.clone.1) | copy-start | bytes 100
  66.9 1.8 copy-start.3
  66.9 1.8 copy-start
  67.0 1.8 copy-start.2
  67.0 1.8 copy-start.5
  67.0 1.8 copy-start.6
  67.0 1.8 copy-start.7
  853.3 1.3 copy-start.1
